TPU v7x, 512 devices: a whole 4x8x8 slice. The times are simulated.
512 devices in a mesh: blk: 16 (over z, y_lo), tan: 32 (over y_hi, x, core).
Axes of the slice: x: 4, y: 8 (y_hi: 4, y_lo: 2; y = y_hi * 2 + y_lo), z: 8, core: 2. Of those that a mesh axis runs over, the one named last changes fastest.
Arguments:
- layer_in: bfloat16 [2048, 256], P('blk'), may hold values from -6 to 6
- laplace_in: bfloat16 [2048, 256], P('blk'), may hold values from -6 to 6
- tangent_in: bfloat16 [2048, 64, 256], P('blk', 'tan'), may hold values from -1.5 to 1.5
- spin_labels: int32 [2048], P('blk'), may hold values from 0 to 1
- pair_bias: bfloat16 [2048, 2048], P('blk'), may hold values from -6 to 306
- query_weight: bfloat16 [256, 256], replicated, may hold values from -0.375 to 0.375
- key_weight: bfloat16 [256, 256], replicated, may hold values from -0.375 to 0.375
- value_weight: bfloat16 [256, 256], replicated, may hold values from -0.375 to 0.375
- out_weight: bfloat16 [256, 256], replicated, may hold values from -0.375 to 0.375
- head_gain: float32 [4], replicated, may hold values from 0.5 to 2
- spin_gain: float32 [4], replicated, may hold values from -2 to 2
Outputs:
- layer_out: bfloat16 [2048, 256], P('blk')
- tangent_out: bfloat16 [2048, 64, 256], P('blk', 'tan')
- laplacian_out: float32 [2048, 256], P('blk')
All inputs are finite; a program needn't handle non-finite values.
Results may differ from a plain program's by a relative error of at most 0.02.
Values may be sent and summed in bfloat16 or wider, within the bound.
A program may use at most 64 MiB of HBM per device.

v0:
```python
import math
import jax
import jax.numpy as jnp
from jax import lax
from jax.sharding import PartitionSpec as P


def project(rows, weight):
    return jnp.dot(rows, weight, preferred_element_type=jnp.float32).astype(jnp.bfloat16)


def project_tangent(tangent, weight):
    count, dirs, width = tangent.shape
    return project(tangent.reshape(count * dirs, width), weight).reshape(count, dirs, width)


def on_device(
    layer_in,
    laplace_in,
    tangent_in,
    spin_labels,
    pair_bias,
    query_weight,
    key_weight,
    value_weight,
    out_weight,
    head_gain,
    spin_gain,
):
    rows, width = layer_in.shape
    heads = head_gain.shape[0]
    head_size = width // heads
    dirs = tangent_in.shape[1]
    scale = 1.0 / math.sqrt(head_size)
    bias_cols = lax.all_to_all(pair_bias, "blk", split_axis=1, concat_axis=0, tiled=True)
    query = project(layer_in, query_weight).reshape(rows, heads, head_size)
    lap_query = project(laplace_in, query_weight).reshape(rows, heads, head_size)
    tan_query = project_tangent(tangent_in, query_weight).reshape(rows, dirs, heads, head_size)
    spin_query = spin_labels.astype(jnp.float32)
    spin_wire = spin_labels.astype(jnp.bfloat16)

    def attend(carry, block, first):
        top, total, numer, tan_total, tan_numer, lap_total, lap_numer, trace_total, trace_numer = (
            carry
        )
        key_b, value_b, lap_key_b, lap_value_b, tan_key_b, tan_value_b, spin_key = block
        count = key_b.shape[0]
        key_h = key_b.reshape(count, heads, head_size)
        value_h = value_b.reshape(count, heads, head_size)
        lap_key_h = lap_key_b.reshape(count, heads, head_size)
        lap_value_h = lap_value_b.reshape(count, heads, head_size)
        tan_key_h = tan_key_b.reshape(count, dirs, heads, head_size)
        tan_value_h = tan_value_b.reshape(count, dirs, heads, head_size)
        bias_rows = lax.dynamic_slice_in_dim(bias_cols, first, count, 0).astype(jnp.float32)
        spin_float = spin_key.astype(jnp.float32)
        same = (
            spin_query[:, None] * spin_float[None, :]
            + (1.0 - spin_query)[:, None] * (1.0 - spin_float)[None, :]
        )
        scores = (
            jnp.einsum("ihd,jhd->hij", query, key_h, preferred_element_type=jnp.float32) * scale
        )
        scores = (
            scores
            + head_gain[:, None, None] * bias_rows.T[None]
            + spin_gain[:, None, None] * same[None]
        )
        new_top = jnp.maximum(top, jnp.max(scores, axis=2))
        shrink = jnp.exp(top - new_top)
        shrink_rows = shrink.T[:, :, None]
        unnorm = jnp.exp(scores - new_top[:, :, None])
        weights = unnorm.astype(jnp.bfloat16)
        total = total * shrink + jnp.sum(unnorm, axis=2)
        numer = numer * shrink_rows + jnp.einsum(
            "hij,jhd->ihd", weights, value_h, preferred_element_type=jnp.float32
        )
        lap_scores = (
            jnp.einsum("ihd,jhd->hij", lap_query, key_h, preferred_element_type=jnp.float32)
            + jnp.einsum("ihd,jhd->hij", query, lap_key_h, preferred_element_type=jnp.float32)
        ) * scale
        lap_weighted = unnorm * lap_scores
        lap_total = lap_total * shrink + jnp.sum(lap_weighted, axis=2)
        lap_numer = (
            lap_numer * shrink_rows
            + jnp.einsum(
                "hij,jhd->ihd",
                lap_weighted.astype(jnp.bfloat16),
                value_h,
                preferred_element_type=jnp.float32,
            )
            + jnp.einsum("hij,jhd->ihd", weights, lap_value_h, preferred_element_type=jnp.float32)
        )
        tan_scores = (
            jnp.einsum("iahd,jhd->ahij", tan_query, key_h, preferred_element_type=jnp.float32)
            + jnp.einsum("ihd,jahd->ahij", query, tan_key_h, preferred_element_type=jnp.float32)
        ) * scale
        cross = (
            jnp.einsum("iahd,jahd->ahij", tan_query, tan_key_h, preferred_element_type=jnp.float32)
            * scale
        )
        tan_weighted = unnorm[None] * tan_scores
        tan_weights = tan_weighted.astype(jnp.bfloat16)
        tan_total = tan_total * shrink[None] + jnp.sum(tan_weighted, axis=3)
        tan_numer = (
            tan_numer * shrink_rows[:, None]
            + jnp.einsum("ahij,jhd->iahd", tan_weights, value_h, preferred_element_type=jnp.float32)
            + jnp.einsum("hij,jahd->iahd", weights, tan_value_h, preferred_element_type=jnp.float32)
        )
        second = unnorm[None] * (tan_scores * tan_scores + 2.0 * cross)
        trace_total = trace_total * shrink + jnp.sum(second, axis=(0, 3))
        trace_numer = (
            trace_numer * shrink_rows
            + jnp.einsum(
                "ahij,jhd->ihd",
                second.astype(jnp.bfloat16),
                value_h,
                preferred_element_type=jnp.float32,
            )
            + 2.0
            * jnp.einsum(
                "ahij,jahd->ihd", tan_weights, tan_value_h, preferred_element_type=jnp.float32
            )
        )
        return (
            new_top,
            total,
            numer,
            tan_total,
            tan_numer,
            lap_total,
            lap_numer,
            trace_total,
            trace_numer,
        )

    head_zeros = jnp.zeros((heads, rows), jnp.float32)
    row_zeros = jnp.zeros((rows, heads, head_size), jnp.float32)
    start_carry = (
        jnp.full((heads, rows), -1e30, jnp.float32),
        head_zeros,
        row_zeros,
        jnp.zeros((dirs, heads, rows), jnp.float32),
        jnp.zeros((rows, dirs, heads, head_size), jnp.float32),
        head_zeros,
        row_zeros,
        head_zeros,
        row_zeros,
    )
    own_keys = project(layer_in, key_weight)
    own_values = project(layer_in, value_weight)
    own_lap_keys = project(laplace_in, key_weight)
    own_lap_values = project(laplace_in, value_weight)
    own_tan_keys = project_tangent(tangent_in, key_weight)
    own_tan_values = project_tangent(tangent_in, value_weight)
    block = (
        lax.all_gather(own_keys, "blk", axis=0, tiled=True),
        lax.all_gather(own_values, "blk", axis=0, tiled=True),
        lax.all_gather(own_lap_keys, "blk", axis=0, tiled=True),
        lax.all_gather(own_lap_values, "blk", axis=0, tiled=True),
        lax.all_gather(own_tan_keys, "blk", axis=0, tiled=True),
        lax.all_gather(own_tan_values, "blk", axis=0, tiled=True),
        lax.all_gather(spin_wire, "blk", axis=0, tiled=True),
    )
    count = block[0].shape[0]
    size = 256
    parts = count // size
    stacked = tuple((piece.reshape((parts, size) + piece.shape[1:]) for piece in block))

    def step(inner, item):
        number, pieces = item
        return (attend(inner, pieces, number * size), None)

    result, _ = lax.scan(step, start_carry, (jnp.arange(parts, dtype=jnp.int32), stacked))
    top, total, numer, tan_total, tan_numer, lap_total, lap_numer, trace_total, trace_numer = result
    denom = total.T[:, :, None]
    denom_sq = denom * denom
    attn = numer / denom
    tan_denom = jnp.transpose(tan_total, (2, 0, 1))[..., None]
    attn_tan = tan_numer / denom[:, None] - numer[:, None] * tan_denom / denom_sq[:, None]
    cross_sum = jnp.sum(tan_numer * tan_denom, axis=1)
    square_sum = jnp.sum(tan_denom * tan_denom, axis=1)
    own_terms = (
        trace_numer / denom
        - numer * trace_total.T[:, :, None] / denom_sq
        - 2.0 * cross_sum / denom_sq
        + 2.0 * numer * square_sum / (denom_sq * denom)
    )
    shared = lax.psum(own_terms.reshape(rows, width).astype(jnp.bfloat16), "tan").astype(
        jnp.float32
    )
    attn_lap = (lap_numer / denom - numer * lap_total.T[:, :, None] / denom_sq).reshape(
        rows, width
    ) + shared
    layer_out = (
        jnp.dot(
            attn.reshape(rows, width).astype(jnp.bfloat16),
            out_weight,
            preferred_element_type=jnp.float32,
        )
        + layer_in.astype(jnp.float32)
    ).astype(jnp.bfloat16)
    tan_flat = attn_tan.reshape(rows * dirs, width).astype(jnp.bfloat16)
    tangent_out = jnp.dot(tan_flat, out_weight, preferred_element_type=jnp.float32).reshape(
        rows, dirs, width
    )
    tangent_out = (tangent_out + tangent_in.astype(jnp.float32)).astype(jnp.bfloat16)
    laplacian_out = jnp.dot(
        attn_lap.astype(jnp.bfloat16), out_weight, preferred_element_type=jnp.float32
    ) + laplace_in.astype(jnp.float32)
    return (layer_out, tangent_out, laplacian_out)


def solution(mesh):
    in_specs = (
        P("blk", None),
        P("blk", None),
        P("blk", "tan", None),
        P("blk"),
        P("blk", None),
        P(),
        P(),
        P(),
        P(),
        P(),
        P(),
    )
    out_specs = (P("blk", None), P("blk", "tan", None), P("blk", None))
    return jax.shard_map(
        on_device, mesh=mesh, in_specs=in_specs, out_specs=out_specs, check_vma=False
    )
```

profile of v0, /device:TPU:8, one launch (start us, length us, event | category | flops | bytes accessed | tf_op | source)
XLA Modules:
  0.0 942.7 jit_solution(8929567075966488008)
XLA Ops:
  7.2 1.8 convolution_convert_fusion.8
  9.1 1.7 convolution_convert_fusion.3
  10.9 1.7 convolution_convert_fusion.6
  12.7 1.7 convolution_convert_fusion.4
  19.4 11.8 %all-to-all-start = ((bf16[128,16,128]{2,0,1:T(8,128)(2,1)}), bf16[128,16,128]{2,0,1:T(8,128)(2,1)}, u32[]{:S(2)}, u32[]{:S(2)}) async-start(bf16[128,16,128]{2,0,1:T(8,128)(2,1)} %copy_bitcast_fusion), calls=%async_computation | async-start | bytes 1048576 | tf_op jit(solution)/shard_map/all_to_all | solution.py:35
  32.5 34.9 %all-gather = bf16[16,1,128]{2,1,0:T(2,128)(2,1)S(1)} all-gather(bf16[1,1,128]{2,1,0:T(2,128)(2,1)S(1)} %get-tuple-element.593), channel_id=1, replica_groups=mesh['blk'=16,'tan'=32] {'blk'}, dimensions={0}, use_global_device_ids=true | all-gather | bytes 4352 | tf_op jit(solution)/shard_map/all_gather | solution.py:162
  69.9 20.5 %all-gather.8.cloned.1.call-done = bf16[2048,256]{1,0:T(8,128)(2,1)} async-done(((bf16[128,256]{1,0:T(8,128)(2,1)}), bf16[2048,256]{1,0:T(8,128)(2,1)}) %all-gather.8.cloned.1.call-update) | async-done | bytes 1048592 | tf_op jit(solution)/shard_map/all_gather | solution.py:156
  90.4 74.6 %all-gather.18.cloned.1.call-done = bf16[2048,256]{1,0:T(8,128)(2,1)} async-done(((bf16[128,256]{1,0:T(8,128)(2,1)}), bf16[2048,256]{1,0:T(8,128)(2,1)}) %all-gather.18.cloned.1.call-update) | async-done | bytes 1048592 | tf_op jit(solution)/shard_map/all_gather | solution.py:159
  165.0 75.4 %all-gather.10.cloned.1.call-done = bf16[2048,256]{1,0:T(8,128)(2,1)} async-done(((bf16[128,256]{1,0:T(8,128)(2,1)}), bf16[2048,256]{1,0:T(8,128)(2,1)}) %all-gather.10.cloned.1.call-update) | async-done | bytes 1048592 | tf_op jit(solution)/shard_map/all_gather | solution.py:157
  240.4 75.2 %all-gather.16.cloned.1.call-done = bf16[2048,256]{1,0:T(8,128)(2,1)} async-done(((bf16[128,256]{1,0:T(8,128)(2,1)}), bf16[2048,256]{1,0:T(8,128)(2,1)}) %all-gather.16.cloned.1.call-update) | async-done | bytes 1048592 | tf_op jit(solution)/shard_map/all_gather | solution.py:158
  315.6 80.3 %all-gather.12.cloned.1.call-done = bf16[2048,2,256]{2,0,1:T(8,128)(2,1)} async-done(((bf16[128,2,256]{2,0,1:T(8,128)(2,1)}), bf16[2048,2,256]{2,0,1:T(8,128)(2,1)}) %all-gather.12.cloned.1.call-update) | async-done | bytes 2097168 | tf_op jit(solution)/shard_map/all_gather | solution.py:160
  395.9 79.9 %all-gather.14.cloned.1.call-done = bf16[2048,2,256]{2,0,1:T(8,128)(2,1)} async-done(((bf16[128,2,256]{2,0,1:T(8,128)(2,1)}), bf16[2048,2,256]{2,0,1:T(8,128)(2,1)}) %all-gather.14.cloned.1.call-update) | async-done | bytes 2097168 | tf_op jit(solution)/shard_map/all_gather | solution.py:161
  476.3 194.2 %while.29 = (s32[]{:T(128)}, f32[4,128]{1,0:T(4,128)S(1)}, f32[4,128]{1,0:T(4,128)}, f32[128,4,64]{0,2,1:T(8,128)}, f32[2,4,128]{2,0,1:T(2,128)S(1)}, /*index=5*...) while((s32[]{:T(128)}, f32[4,128]{1,0:T(4,128)S(1)}, ...), condition=%wide.region_7.8_spmd.clone, body=%wide.region_0.7_spmd.clone.sunk | while | flops 325065856 | bytes 26266780 | solution.py:173
  479.9 1.6 constant_dynamic-slice_fusion.10
  486.1 1.5 multiply_convert_fusion.2
  488.6 1.4 convert_reduce_fusion.2
  491.5 1.7 fusion.155
  499.9 1.2 dynamic_slice.87
  503.5 1.6 constant_dynamic-slice_fusion.10
  509.7 1.5 multiply_convert_fusion.2
  512.3 1.4 convert_reduce_fusion.2
  515.8 1.8 fusion.155
  527.9 1.6 constant_dynamic-slice_fusion.10
  534.1 1.5 multiply_convert_fusion.2
  536.6 1.4 convert_reduce_fusion.2
  540.2 1.8 fusion.155
  552.2 1.6 constant_dynamic-slice_fusion.10
  558.5 1.5 multiply_convert_fusion.2
  561.0 1.4 convert_reduce_fusion.2
  564.6 1.8 fusion.155
  576.6 1.6 constant_dynamic-slice_fusion.10
  582.8 1.5 multiply_convert_fusion.2
  585.4 1.4 convert_reduce_fusion.2
  589.0 1.8 fusion.155
  601.0 1.6 constant_dynamic-slice_fusion.10
  607.2 1.5 multiply_convert_fusion.2
  609.7 1.4 convert_reduce_fusion.2
  613.3 1.8 fusion.155
  625.4 1.6 constant_dynamic-slice_fusion.10
  631.6 1.5 multiply_convert_fusion.2
  634.1 1.4 convert_reduce_fusion.2
  637.7 1.8 fusion.155
  649.7 1.6 constant_dynamic-slice_fusion.10
  655.9 1.5 multiply_convert_fusion.2
  658.5 1.4 convert_reduce_fusion.2
  662.1 1.8 fusion.155
  672.4 1.8 add_convert_fusion
  677.1 257.1 %all-reduce.2.cloned.1.call-done = bf16[128,256]{0,1:T(8,128)(2,1)} async-done(((bf16[128,256]{0,1:T(8,128)(2,1)}), bf16[128,256]{0,1:T(8,128)(2,1)}) %all-reduce.2.cloned.1.call-update) | async-done | bytes 65552 | tf_op jit(solution)/shard_map/psum | solution.py:188
  (469 shorter events, 151.2 us)
Async XLA Ops:
  7.2 11.3 %copy-start = (bf16[128,2048]{1,0:T(8,128)(2,1)S(1)}, bf16[128,2048]{1,0:T(8,128)(2,1)}, u32[]{:S(2)}) copy-start(bf16[128,2048]{1,0:T(8,128)(2,1)} %param.17) | copy-start | bytes 1572868
  7.2 10.3 %copy-start.5 = (bf16[256,256]{1,0:T(8,128)(2,1)S(1)}, bf16[256,256]{1,0:T(8,128)(2,1)}, u32[]{:S(2)}) copy-start(bf16[256,256]{1,0:T(8,128)(2,1)} %param.20) | copy-start | bytes 393220
  7.2 83.2 %all-gather.8.cloned.1.call-start = ((), (), s32[]{:S(2)}) async-start(), calls=%async_computation.1 | async-start | bytes 1114112 | tf_op jit(solution)/shard_map/all_gather | solution.py:156
  9.1 155.9 %all-gather.18.cloned.1.call-start = ((), (), s32[]{:S(2)}) async-start(), calls=%async_computation.6 | async-start | bytes 1114112 | tf_op jit(solution)/shard_map/all_gather | solution.py:159
  10.9 229.5 %all-gather.10.cloned.1.call-start = ((), (), s32[]{:S(2)}) async-start(), calls=%async_computation.2 | async-start | bytes 1114112 | tf_op jit(solution)/shard_map/all_gather | solution.py:157
  12.7 302.9 %all-gather.16.cloned.1.call-start = ((), (), s32[]{:S(2)}) async-start(), calls=%async_computation.5 | async-start | bytes 1114112 | tf_op jit(solution)/shard_map/all_gather | solution.py:158
  14.5 381.4 %all-gather.12.cloned.1.call-start = ((), (), s32[]{:S(2)}) async-start(), calls=%async_computation.3 | async-start | bytes 2228224 | tf_op jit(solution)/shard_map/all_gather | solution.py:160
  15.5 15.8 %copy-start.6 = (bf16[256,256]{1,0:T(8,128)(2,1)S(1)}, bf16[256,256]{1,0:T(8,128)(2,1)}, u32[]{:S(2)}) copy-start(bf16[256,256]{1,0:T(8,128)(2,1)} %param.18) | copy-start | bytes 393220
  17.4 15.1 %copy-start.18 = (s32[128]{0:T(128)S(1)}, s32[128]{0:T(128)}, u32[]{:S(2)}) copy-start(s32[128]{0:T(128)} %param.16) | copy-start | bytes 1540
  17.4 50.7 %copy-start.8 = (bf16[128,256]{1,0:T(8,128)(2,1)S(1)}, bf16[128,256]{1,0:T(8,128)(2,1)}, u32[]{:S(2)}) copy-start(bf16[128,256]{1,0:T(8,128)(2,1)} %param.13) | copy-start | bytes 196612
  17.4 458.3 %all-gather.14.cloned.1.call-start = ((), (), s32[]{:S(2)}) async-start(), calls=%async_computation.4 | async-start | bytes 2228224 | tf_op jit(solution)/shard_map/all_gather | solution.py:161
  17.8 51.2 %copy-start.10 = (bf16[128,256]{1,0:T(8,128)(2,1)S(1)}, bf16[128,256]{1,0:T(8,128)(2,1)}, u32[]{:S(2)}) copy-start(bf16[128,256]{1,0:T(8,128)(2,1)} %param.14) | copy-start | bytes 196612
  19.4 50.5 %all-to-all-start = ((bf16[128,16,128]{2,0,1:T(8,128)(2,1)}), bf16[128,16,128]{2,0,1:T(8,128)(2,1)}, u32[]{:S(2)}, u32[]{:S(2)}) async-start(bf16[128,16,128]{2,0,1:T(8,128)(2,1)} %copy_bitcast_fusion), calls=%async_computation | async-start | bytes 1048576 | tf_op jit(solution)/shard_map/all_to_all | solution.py:35
  31.2 902.9 %all-reduce.2.cloned.1.call-start = ((), (), s32[]{:S(2)}) async-start(), calls=%async_computation.7 | async-start | bytes 131072 | tf_op jit(solution)/shard_map/psum | solution.py:188
  476.3 5.2 copy-start.16
  490.0 6.7 copy-start.4
  494.4 3.5 copy-start.1
  499.9 5.2 copy-start.16
  513.6 7.5 copy-start.4
  518.8 3.5 copy-start.1
  521.1 2.3 copy-start.2
  524.3 5.2 copy-start.16
  538.0 7.5 copy-start.4
  543.1 3.5 copy-start.1
  545.5 2.3 copy-start.2
  548.7 5.2 copy-start.16
  562.4 7.5 copy-start.4
  567.5 3.5 copy-start.1
  569.8 2.3 copy-start.2
  573.1 5.2 copy-start.16
  586.7 7.5 copy-start.4
  591.9 3.5 copy-start.1
  594.2 2.3 copy-start.2
  597.4 5.2 copy-start.16
  611.1 7.5 copy-start.4
  616.2 3.5 copy-start.1
  618.6 2.3 copy-start.2
  621.8 5.2 copy-start.16
  635.5 7.5 copy-start.4
  640.6 3.5 copy-start.1
  642.9 2.3 copy-start.2
  646.2 5.2 copy-start.16
  659.8 7.5 copy-start.4
  665.0 3.5 copy-start.1
  667.3 2.3 copy-start.2
  670.5 4.9 copy-start.7
  670.5 4.9 copy-start.9
  670.5 264.5 %copy-start.11 = (bf16[128,256]{1,0:T(8,128)(2,1)S(1)}, bf16[128,256]{1,0:T(8,128)(2,1)}, u32[]{:S(2)}) copy-start(bf16[128,256]{1,0:T(8,128)(2,1)} %param.14) | copy-start | bytes 196612
  (49 other events, 56.8 us)
Sparse Core Ops, SparseCore 0:
  10.7 79.6 all-gather.7
  92.5 72.4 all-gather.17
  167.1 73.2 all-gather.9
  242.3 73.2 all-gather.15
  317.5 78.3 all-gather.11
  397.8 77.8 all-gather.13
  674.3 259.7 all-reduce.1
where the time goes:
time: 947 us; the launch traced here: 943 us
  waiting for transfers between devices  663 us (70%)
  matrix products  112 us (12%)
  local copies, waits for them, and re-layouts  65 us (7%)
  blocking collectives  34.9 us (4%)
  other arithmetic  34.7 us (4%)
  between operations  14.4 us (2%)
  starting transfers between devices  12.1 us (1%)
    psum x1, waiting for transfers between devices, on_device(): lax.psum(own_terms.reshape(rows, width).astype(jnp.bfloat16), 'tan')  257 us
    all_gather x1, waiting for transfers between devices, on_device(): lax.all_gather(own_tan_keys, 'blk', axis=0, tiled=True)  80.3 us
    all_gather x1, waiting for transfers between devices, on_device(): lax.all_gather(own_tan_values, 'blk', axis=0, tiled=True)  79.9 us
    all_gather x1, waiting for transfers between devices, on_device(): lax.all_gather(own_values, 'blk', axis=0, tiled=True)  75.4 us
    all_gather x1, waiting for transfers between devices, on_device(): lax.all_gather(own_lap_keys, 'blk', axis=0, tiled=True)  75.2 us
    all_gather x1, waiting for transfers between devices, on_device(): lax.all_gather(own_lap_values, 'blk', axis=0, tiled=True)  74.6 us
    dynamic_slice x80, local copies, waits for them, and re-layouts, on_device(): lax.scan(step, start_carry, (jnp.arange(parts, dtype=jnp.int32), stacked))  52.4 us
    all_gather x1, blocking collectives, on_device(): lax.all_gather(spin_wire, 'blk', axis=0, tiled=True)  34.9 us
  transfers between devices with their start and end apart: 8, of which 7 were waited for; matrix products, arithmetic and copies ran while one was open for 2% of the time, Pallas kernels for 0%

commit v1 on v0

--- a/solution.py
+++ b/solution.py
@@ -185,9 +185,9 @@
         - 2.0 * cross_sum / denom_sq
         + 2.0 * numer * square_sum / (denom_sq * denom)
     )
-    shared = lax.psum(own_terms.reshape(rows, width).astype(jnp.bfloat16), "tan").astype(
-        jnp.float32
-    )
+    shared = jnp.sum(
+        lax.all_gather(own_terms.reshape(rows, width).astype(jnp.bfloat16), "tan"), axis=0
+    ).astype(jnp.float32)
     attn_lap = (lap_numer / denom - numer * lap_total.T[:, :, None] / denom_sq).reshape(
         rows, width
     ) + shared

time: 947 us -> 749 us (0.79)
  the two profiles are of different devices: /device:TPU:8 before, /device:TPU:1 now
where the time goes in v1:
time: 749 us; the launch traced here: 745 us
  waiting for transfers between devices  467 us (62%)
  matrix products  112 us (15%)
  local copies, waits for them, and re-layouts  65.8 us (9%)
  other arithmetic  35.1 us (5%)
  blocking collectives  31.1 us (4%)
  between operations  14.4 us (2%)
  starting transfers between devices  12.3 us (2%)
    all_gather x1, waiting for transfers between devices, on_device(): lax.all_gather(own_tan_keys, 'blk', axis=0, tiled=True)  81.3 us
    all_gather x1, waiting for transfers between devices, on_device(): lax.all_gather(own_tan_values, 'blk', axis=0, tiled=True)  79.9 us
    all_gather x1, waiting for transfers between devices, on_device(): lax.all_gather(own_values, 'blk', axis=0, tiled=True)  75.4 us
    all_gather x1, waiting for transfers between devices, on_device(): lax.all_gather(own_lap_keys, 'blk', axis=0, tiled=True)  75.2 us
    all_gather x1, waiting for transfers between devices, on_device(): lax.all_gather(own_lap_values, 'blk', axis=0, tiled=True)  74.7 us
    all_gather x1, waiting for transfers between devices, on_device(): lax.all_gather(own_terms.reshape(rows, width).astype(jnp.bfloat16), 'tan')  65.7 us
    dynamic_slice x80, local copies, waits for them, and re-layouts, on_device(): lax.scan(step, start_carry, (jnp.arange(parts, dtype=jnp.int32), stacked))  52.4 us
    all_gather x1, blocking collectives, on_device(): lax.all_gather(spin_wire, 'blk', axis=0, tiled=True)  31.1 us
  transfers between devices with their start and end apart: 8, of which 7 were waited for; matrix products, arithmetic and copies ran while one was open for 2% of the time, Pallas kernels for 0%

profile of v1, /device:TPU:1, one launch (start us, length us, event | category | flops | bytes accessed | tf_op | source)
XLA Modules:
  0.0 744.7 jit_solution(13933188146281048087)
XLA Ops:
  7.2 1.8 convolution_convert_fusion.8
  9.1 1.7 convolution_convert_fusion.3
  10.9 1.7 convolution_convert_fusion.6
  12.7 1.7 convolution_convert_fusion.4
  19.4 12.0 %all-to-all-start = ((bf16[128,16,128]{2,0,1:T(8,128)(2,1)}), bf16[128,16,128]{2,0,1:T(8,128)(2,1)}, u32[]{:S(2)}, u32[]{:S(2)}) async-start(bf16[128,16,128]{2,0,1:T(8,128)(2,1)} %copy_bitcast_fusion), calls=%async_computation | async-start | bytes 1048576 | tf_op jit(solution)/shard_map/all_to_all | solution.py:35
  32.8 31.1 %all-gather = bf16[16,1,128]{2,1,0:T(2,128)(2,1)S(1)} all-gather(bf16[1,1,128]{2,1,0:T(2,128)(2,1)S(1)} %get-tuple-element.677), channel_id=1, replica_groups=mesh['blk'=16,'tan'=32] {'blk'}, dimensions={0}, use_global_device_ids=true | all-gather | bytes 4352 | tf_op jit(solution)/shard_map/all_gather | solution.py:162
  66.3 15.1 %all-gather.9.cloned.1.call-done = bf16[2048,256]{1,0:T(8,128)(2,1)} async-done(((bf16[128,256]{1,0:T(8,128)(2,1)}), bf16[2048,256]{1,0:T(8,128)(2,1)}) %all-gather.9.cloned.1.call-update) | async-done | bytes 1048592 | tf_op jit(solution)/shard_map/all_gather | solution.py:156
  81.4 74.7 %all-gather.19.cloned.1.call-done = bf16[2048,256]{1,0:T(8,128)(2,1)} async-done(((bf16[128,256]{1,0:T(8,128)(2,1)}), bf16[2048,256]{1,0:T(8,128)(2,1)}) %all-gather.19.cloned.1.call-update) | async-done | bytes 1048592 | tf_op jit(solution)/shard_map/all_gather | solution.py:159
  156.1 75.4 %all-gather.11.cloned.1.call-done = bf16[2048,256]{1,0:T(8,128)(2,1)} async-done(((bf16[128,256]{1,0:T(8,128)(2,1)}), bf16[2048,256]{1,0:T(8,128)(2,1)}) %all-gather.11.cloned.1.call-update) | async-done | bytes 1048592 | tf_op jit(solution)/shard_map/all_gather | solution.py:157
  231.5 75.2 %all-gather.17.cloned.1.call-done = bf16[2048,256]{1,0:T(8,128)(2,1)} async-done(((bf16[128,256]{1,0:T(8,128)(2,1)}), bf16[2048,256]{1,0:T(8,128)(2,1)}) %all-gather.17.cloned.1.call-update) | async-done | bytes 1048592 | tf_op jit(solution)/shard_map/all_gather | solution.py:158
  306.7 81.3 %all-gather.13.cloned.1.call-done = bf16[2048,2,256]{2,0,1:T(8,128)(2,1)} async-done(((bf16[128,2,256]{2,0,1:T(8,128)(2,1)}), bf16[2048,2,256]{2,0,1:T(8,128)(2,1)}) %all-gather.13.cloned.1.call-update) | async-done | bytes 2097168 | tf_op jit(solution)/shard_map/all_gather | solution.py:160
  388.0 79.9 %all-gather.15.cloned.1.call-done = bf16[2048,2,256]{2,0,1:T(8,128)(2,1)} async-done(((bf16[128,2,256]{2,0,1:T(8,128)(2,1)}), bf16[2048,2,256]{2,0,1:T(8,128)(2,1)}) %all-gather.15.cloned.1.call-update) | async-done | bytes 2097168 | tf_op jit(solution)/shard_map/all_gather | solution.py:161
  468.4 194.3 %while.29 = (s32[]{:T(128)}, f32[4,128]{1,0:T(4,128)S(1)}, f32[4,128]{1,0:T(4,128)}, f32[128,4,64]{0,2,1:T(8,128)}, f32[2,4,128]{2,0,1:T(2,128)S(1)}, /*index=5*...) while((s32[]{:T(128)}, f32[4,128]{1,0:T(4,128)S(1)}, ...), condition=%wide.region_7.8_spmd.clone, body=%wide.region_0.7_spmd.clone.sunk | while | flops 325065856 | bytes 26266780 | solution.py:173
  471.9 1.6 constant_dynamic-slice_fusion.10
  478.2 1.5 multiply_convert_fusion.2
  480.7 1.4 convert_reduce_fusion.2
  483.6 1.7 fusion.153
  495.6 1.6 constant_dynamic-slice_fusion.10
  501.8 1.5 multiply_convert_fusion.2
  504.3 1.4 convert_reduce_fusion.2
  507.9 1.8 fusion.153
  516.4 1.2 dynamic_slice.87
  520.0 1.6 constant_dynamic-slice_fusion.10
  526.2 1.5 multiply_convert_fusion.2
  528.7 1.4 convert_reduce_fusion.2
  532.3 1.8 fusion.153
  544.3 1.6 constant_dynamic-slice_fusion.10
  550.5 1.5 multiply_convert_fusion.2
  553.1 1.4 convert_reduce_fusion.2
  556.7 1.8 fusion.153
  568.7 1.6 constant_dynamic-slice_fusion.10
  574.9 1.5 multiply_convert_fusion.2
  577.5 1.4 convert_reduce_fusion.2
  581.0 1.8 fusion.153
  593.1 1.6 constant_dynamic-slice_fusion.10
  599.3 1.5 multiply_convert_fusion.2
  601.8 1.4 convert_reduce_fusion.2
  605.4 1.8 fusion.153
  617.5 1.6 constant_dynamic-slice_fusion.10
  623.7 1.5 multiply_convert_fusion.2
  626.2 1.4 convert_reduce_fusion.2
  629.8 1.8 fusion.153
  641.8 1.6 constant_dynamic-slice_fusion.10
  648.0 1.5 multiply_convert_fusion.2
  650.6 1.4 convert_reduce_fusion.2
  654.2 1.8 fusion.153
  669.4 65.7 %all-gather.21.cloned.1.call-done = bf16[32,128,256]{2,1,0:T(8,128)(2,1)} async-done(((bf16[1,128,256]{2,1,0:T(8,128)(2,1)}), bf16[32,128,256]{2,1,0:T(8,128)(2,1)}) %all-gather.21.cloned.1.call-update) | async-done | bytes 2097168 | tf_op jit(solution)/shard_map/all_gather | solution.py:189
  735.1 1.9 reduce_sum.92
  (471 shorter events, 152.3 us)
Async XLA Ops:
  7.2 11.3 %copy-start = (bf16[128,2048]{1,0:T(8,128)(2,1)S(1)}, bf16[128,2048]{1,0:T(8,128)(2,1)}, u32[]{:S(2)}) copy-start(bf16[128,2048]{1,0:T(8,128)(2,1)} %param.17) | copy-start | bytes 1572868
  7.2 10.3 %copy-start.5 = (bf16[256,256]{1,0:T(8,128)(2,1)S(1)}, bf16[256,256]{1,0:T(8,128)(2,1)}, u32[]{:S(2)}) copy-start(bf16[256,256]{1,0:T(8,128)(2,1)} %param.20) | copy-start | bytes 393220
  7.2 74.2 %all-gather.9.cloned.1.call-start = ((), (), s32[]{:S(2)}) async-start(), calls=%async_computation.1 | async-start | bytes 1114112 | tf_op jit(solution)/shard_map/all_gather | solution.py:156
  9.1 147.0 %all-gather.19.cloned.1.call-start = ((), (), s32[]{:S(2)}) async-start(), calls=%async_computation.6 | async-start | bytes 1114112 | tf_op jit(solution)/shard_map/all_gather | solution.py:159
  10.9 220.6 %all-gather.11.cloned.1.call-start = ((), (), s32[]{:S(2)}) async-start(), calls=%async_computation.2 | async-start | bytes 1114112 | tf_op jit(solution)/shard_map/all_gather | solution.py:157
  12.7 294.0 %all-gather.17.cloned.1.call-start = ((), (), s32[]{:S(2)}) async-start(), calls=%async_computation.5 | async-start | bytes 1114112 | tf_op jit(solution)/shard_map/all_gather | solution.py:158
  14.5 373.5 %all-gather.13.cloned.1.call-start = ((), (), s32[]{:S(2)}) async-start(), calls=%async_computation.3 | async-start | bytes 2228224 | tf_op jit(solution)/shard_map/all_gather | solution.py:160
  15.5 16.1 %copy-start.6 = (bf16[256,256]{1,0:T(8,128)(2,1)S(1)}, bf16[256,256]{1,0:T(8,128)(2,1)}, u32[]{:S(2)}) copy-start(bf16[256,256]{1,0:T(8,128)(2,1)} %param.18) | copy-start | bytes 393220
  17.4 15.4 %copy-start.18 = (s32[128]{0:T(128)S(1)}, s32[128]{0:T(128)}, u32[]{:S(2)}) copy-start(s32[128]{0:T(128)} %param.16) | copy-start | bytes 1540
  17.4 47.1 %copy-start.8 = (bf16[128,256]{1,0:T(8,128)(2,1)S(1)}, bf16[128,256]{1,0:T(8,128)(2,1)}, u32[]{:S(2)}) copy-start(bf16[128,256]{1,0:T(8,128)(2,1)} %param.13) | copy-start | bytes 196612
  17.4 450.4 %all-gather.15.cloned.1.call-start = ((), (), s32[]{:S(2)}) async-start(), calls=%async_computation.4 | async-start | bytes 2228224 | tf_op jit(solution)/shard_map/all_gather | solution.py:161
  17.8 47.7 %copy-start.10 = (bf16[128,256]{1,0:T(8,128)(2,1)S(1)}, bf16[128,256]{1,0:T(8,128)(2,1)}, u32[]{:S(2)}) copy-start(bf16[128,256]{1,0:T(8,128)(2,1)} %param.14) | copy-start | bytes 196612
  19.4 46.9 %all-to-all-start = ((bf16[128,16,128]{2,0,1:T(8,128)(2,1)}), bf16[128,16,128]{2,0,1:T(8,128)(2,1)}, u32[]{:S(2)}, u32[]{:S(2)}) async-start(bf16[128,16,128]{2,0,1:T(8,128)(2,1)} %copy_bitcast_fusion), calls=%async_computation | async-start | bytes 1048576 | tf_op jit(solution)/shard_map/all_to_all | solution.py:35
  31.4 703.7 %all-gather.21.cloned.1.call-start = ((), (), s32[]{:S(2)}) async-start(), calls=%async_computation.7 | async-start | bytes 2162688 | tf_op jit(solution)/shard_map/all_gather | solution.py:189
  468.4 5.2 copy-start.16
  482.1 6.7 copy-start.4
  486.5 3.5 copy-start.1
  492.0 5.2 copy-start.16
  505.7 7.5 %copy-start.4 = (f32[128,4,64]{0,2,1:T(8,128)S(1)}, f32[128,4,64]{0,2,1:T(8,128)}, u32[]{:S(2)}) copy-start(f32[128,4,64]{0,2,1:T(8,128)} %get-tuple-element.916) | copy-start | bytes 393220 | tf_op jit(solution)/shard_map/while
  510.9 3.5 copy-start.1
  513.2 2.3 copy-start.2
  516.4 5.2 copy-start.16
  530.1 7.5 %copy-start.4 = (f32[128,4,64]{0,2,1:T(8,128)S(1)}, f32[128,4,64]{0,2,1:T(8,128)}, u32[]{:S(2)}) copy-start(f32[128,4,64]{0,2,1:T(8,128)} %get-tuple-element.916) | copy-start | bytes 393220 | tf_op jit(solution)/shard_map/while
  535.2 3.5 copy-start.1
  537.5 2.3 copy-start.2
  540.8 5.2 copy-start.16
  554.5 7.5 %copy-start.4 = (f32[128,4,64]{0,2,1:T(8,128)S(1)}, f32[128,4,64]{0,2,1:T(8,128)}, u32[]{:S(2)}) copy-start(f32[128,4,64]{0,2,1:T(8,128)} %get-tuple-element.916) | copy-start | bytes 393220 | tf_op jit(solution)/shard_map/while
  559.6 3.5 copy-start.1
  561.9 2.3 copy-start.2
  565.1 5.2 copy-start.16
  578.8 7.5 %copy-start.4 = (f32[128,4,64]{0,2,1:T(8,128)S(1)}, f32[128,4,64]{0,2,1:T(8,128)}, u32[]{:S(2)}) copy-start(f32[128,4,64]{0,2,1:T(8,128)} %get-tuple-element.916) | copy-start | bytes 393220 | tf_op jit(solution)/shard_map/while
  584.0 3.5 copy-start.1
  586.3 2.3 copy-start.2
  589.5 5.2 copy-start.16
  603.2 7.5 %copy-start.4 = (f32[128,4,64]{0,2,1:T(8,128)S(1)}, f32[128,4,64]{0,2,1:T(8,128)}, u32[]{:S(2)}) copy-start(f32[128,4,64]{0,2,1:T(8,128)} %get-tuple-element.916) | copy-start | bytes 393220 | tf_op jit(solution)/shard_map/while
  608.3 3.5 copy-start.1
  610.7 2.3 copy-start.2
  613.9 5.2 copy-start.16
  627.6 7.5 %copy-start.4 = (f32[128,4,64]{0,2,1:T(8,128)S(1)}, f32[128,4,64]{0,2,1:T(8,128)}, u32[]{:S(2)}) copy-start(f32[128,4,64]{0,2,1:T(8,128)} %get-tuple-element.916) | copy-start | bytes 393220 | tf_op jit(solution)/shard_map/while
  632.7 3.5 copy-start.1
  635.0 2.3 copy-start.2
  638.3 5.2 copy-start.16
  651.9 7.5 %copy-start.4 = (f32[128,4,64]{0,2,1:T(8,128)S(1)}, f32[128,4,64]{0,2,1:T(8,128)}, u32[]{:S(2)}) copy-start(f32[128,4,64]{0,2,1:T(8,128)} %get-tuple-element.916) | copy-start | bytes 393220 | tf_op jit(solution)/shard_map/while
  657.1 3.5 copy-start.1
  659.4 2.3 copy-start.2
  662.6 5.9 copy-start.7
  662.6 5.9 copy-start.9
  664.5 72.5 %copy-start.11 = (bf16[128,256]{1,0:T(8,128)(2,1)S(1)}, bf16[128,256]{1,0:T(8,128)(2,1)}, u32[]{:S(2)}) copy-start(bf16[128,256]{1,0:T(8,128)(2,1)} %param.14) | copy-start | bytes 196612
  (49 other events, 56.8 us)
Sparse Core Ops, SparseCore 0:
  10.7 70.6 all-gather.8
  83.5 72.5 all-gather.18
  158.2 73.2 all-gather.10
  233.4 73.2 all-gather.16
  308.6 79.3 all-gather.12
  389.9 77.8 all-gather.14
  666.6 68.5 all-gather.20
